TPU v7x, 32 devices: a whole 2x2x4 slice. The times are simulated.
32 devices in a mesh: sub: 4 (over x, core), tile: 8 (over z, y).
Axes of the slice: x: 2, y: 2, z: 4, core: 2. Of those that a mesh axis runs over, the one named last changes fastest.
Arguments:
- states: float32 [4, 3, 256, 2048], P('sub', None, 'tile'), may hold values from -6 to 6
- terrain: int32 [256, 2048], P('tile'), may hold values from 0 to 7
- depth_table: float32 [8], replicated, may hold values from 0.5 to 2
- spread_table: float32 [8], replicated, may hold values from 0.03 to 0.24
- mixing: float32 [4, 4], replicated, may hold values from -0.9 to 2, as said below
Outputs:
- gradient: float32 [4, 3, 256, 2048], P('sub', None, 'tile')
Inputs may be any that keep to these rules, and one draw needn't show every extreme that they name: `mixing`: A dense matrix with diagonal entries between 1 and 2.
All inputs are finite; a program needn't handle non-finite values.
Results may differ from a plain program's by a relative error of at most 0.00012.
Values sent between devices are 32-bit elements; how exact they have to be, the bound alone decides.
A program may use at most 64 MiB of HBM per device.

v0:
```python
import jax
import jax.numpy as jnp
from jax import lax
from jax.sharding import PartitionSpec as P

FSTEPS = 3
DSTEPS = 3


time_step = 0.5
gravity = 1.0
coriolis = 0.3


def with_halo(value, sides, width):
    for axis, dim in sides:
        peers, length = (lax.axis_size(axis), value.shape[dim])
        up = [(i, (i + 1) % peers) for i in range(peers - 1)]
        down = [(j, i) for i, j in up]
        last = lax.slice_in_dim(value, length - width, length, axis=dim)
        first = lax.slice_in_dim(value, 0, width, axis=dim)
        before = lax.ppermute(last, axis, up)
        after = lax.ppermute(first, axis, down)
        value = jnp.concatenate([before, value, after], axis=dim)
    return value


def passed_along(value, axis, by):
    peers = lax.axis_size(axis)
    pairs = [(i, i + by) for i in range(peers) if 0 <= i + by < peers]
    return lax.ppermute(value, axis, pairs)


def col_diff(field):
    return (jnp.roll(field, -1, -1) - jnp.roll(field, 1, -1)) * 0.5


def row_mask(first, count, total):
    index = first + jnp.arange(count, dtype=jnp.int32)
    return ((index >= 0) & (index < total)).astype(jnp.float32)[:, None]


def crop_rows(field, keep, have):
    cut = have - keep
    if cut == 0:
        return field
    return field[cut : field.shape[0] - cut]


def model_step(state, depth, first, total):
    height, east, north = (state[0], state[1], state[2])
    flux_x = depth * east
    flux_y = depth * north
    new_h = height[1:-1] - time_step * ((flux_x[2:] - flux_x[:-2]) * 0.5 + col_diff(flux_y[1:-1]))
    new_h = new_h * row_mask(first + 1, new_h.shape[0], total)
    new_u = (
        east[2:-2]
        - time_step * gravity * (new_h[2:] - new_h[:-2]) * 0.5
        + time_step * coriolis * north[2:-2]
    )
    new_v = (
        north[2:-2]
        - time_step * gravity * col_diff(new_h[1:-1])
        - time_step * coriolis * east[2:-2]
    )
    result = jnp.stack([new_h[1:-1], new_u, new_v])
    return result * row_mask(first + 2, result.shape[1], total)


def spread_step(field, kappa, first, total):
    centre = field[:, 1:-1]
    laplace = (
        field[:, 2:]
        + field[:, :-2]
        + jnp.roll(centre, 1, 2)
        + jnp.roll(centre, -1, 2)
        - 4.0 * centre
    )
    return (centre + kappa * laplace) * row_mask(first + 1, centre.shape[1], total)


def local(states, terrain, depth_table, spread_table, mixing):
    state = states[0]
    rows = state.shape[1]
    total = rows * lax.axis_size("tile")
    anchor = lax.axis_index("tile") * rows
    classes = jnp.arange(depth_table.shape[0], dtype=jnp.int32)
    pick = (terrain[None] == classes[:, None, None]).astype(jnp.float32)
    coeffs = jnp.stack(
        [
            jnp.sum(pick * depth_table[:, None, None], 0),
            jnp.sum(pick * spread_table[:, None, None], 0),
        ]
    )
    wide = with_halo(coeffs, (("tile", 1),), 6)
    depth_wide = wide[0]
    kappa_wide = wide[1]
    padded = with_halo(state, (("tile", 1),), 6)
    have = 6
    for step in range(FSTEPS):
        padded = model_step(padded, crop_rows(depth_wide, have, 6), anchor - have, total)
        have = have - 2
    state = padded
    earlier = passed_along(state, "sub", 1)
    jumps = states[0] - earlier
    mixed_parts = jnp.einsum(
        "st,tfxy->sfxy",
        mixing,
        lax.all_to_all(jumps[None], "sub", split_axis=3, concat_axis=0, tiled=True),
        precision=lax.Precision.HIGHEST,
    )
    mixed = lax.all_to_all(mixed_parts, "sub", split_axis=0, concat_axis=3, tiled=True)[0]
    field = mixed
    padded = with_halo(field, (("tile", 1),), 3)
    have = 3
    for step in range(DSTEPS):
        padded = spread_step(padded, crop_rows(kappa_wide, have - 1, 6), anchor - have, total)
        have = have - 1
    field = padded
    return field[None]


def solution(mesh):
    in_specs = (P("sub", None, "tile", None), P("tile", None), P(), P(), P())
    out_specs = P("sub", None, "tile", None)
    return jax.shard_map(local, mesh=mesh, in_specs=in_specs, out_specs=out_specs, check_vma=False)
```

profile of v0, /device:TPU:0, one launch (start us, length us, event | category | flops | bytes accessed | tf_op | source)
XLA Modules:
  0.0 125.9 jit_solution(13169863783737920210)
XLA Ops:
  0.0 1.1 fusion.68
  1.1 5.0 %collective-permute-start = (f32[3,6,2048]{2,1,0:T(8,128)S(1)}, f32[3,6,2048]{2,1,0:T(8,128)S(1)}, u32[]{:S(2)}, u32[]{:S(2)}) collective-permute-start(f32[3,6,2048]{2,1,0:T(8,128)S(1)} %get-tuple-element.26), channel_id=1, source_target_pairs={{0,1},{1,2},{2,3},{3,4},{4,5},{5,6},{6,7},{8,9},{9,10},{10,11},{11... | collective-permute-start | bytes 442376 | tf_op jit(solution)/shard_map/ppermute | solution.py:22
  6.1 1.3 %collective-permute-start.1 = (f32[3,6,2048]{2,1,0:T(8,128)S(1)}, f32[3,6,2048]{2,1,0:T(8,128)S(1)}, u32[]{:S(2)}, u32[]{:S(2)}) collective-permute-start(f32[3,6,2048]{2,1,0:T(8,128)S(1)} %get-tuple-element.27), channel_id=1, source_target_pairs={{1,0},{2,1},{3,2},{4,3},{5,4},{6,5},{7,6},{9,8},{10,9},{11,10},{12... | collective-permute-start | bytes 442376 | tf_op jit(solution)/shard_map/ppermute | solution.py:23
  7.4 1.4 %select_reduce_fusion.1 = (f32[32,2048]{1,0:T(8,128)S(1)}, f32[32,2048]{1,0:T(8,128)S(1)}) fusion(f32[8]{0:T(128)} %param.7, s32[32,2048]{1,0:T(8,128)} %param.6, f32[8]{0:T(128)} %param.8), kind=kLoop, calls=%fused_computation.1 | loop fusion | flops 2490368 | bytes 786496 | tf_op jit(solution)/shard_map/reduce_sum | solution.py:91
  9.0 1.3 %collective-permute-start.3 = (f32[2,6,2048]{2,0,1:T(2,128)S(1)}, f32[2,6,2048]{2,0,1:T(2,128)S(1)}, u32[]{:S(2)}, u32[]{:S(2)}) collective-permute-start(f32[2,6,2048]{2,0,1:T(2,128)S(1)} %copy.116), channel_id=1, source_target_pairs={{1,0},{2,1},{3,2},{4,3},{5,4},{6,5},{7,6},{9,8},{10,9},{11,10},{12... | collective-permute-start | bytes 294920 | tf_op jit(solution)/shard_map/ppermute | solution.py:23
  10.4 5.2 %collective-permute-start.2 = (f32[2,6,2048]{2,0,1:T(2,128)S(1)}, f32[2,6,2048]{2,0,1:T(2,128)S(1)}, u32[]{:S(2)}, u32[]{:S(2)}) collective-permute-start(f32[2,6,2048]{2,0,1:T(2,128)S(1)} %copy.115), channel_id=1, source_target_pairs={{0,1},{1,2},{2,3},{3,4},{4,5},{5,6},{6,7},{8,9},{9,10},{10,11},{11... | collective-permute-start | bytes 294920 | tf_op jit(solution)/shard_map/ppermute | solution.py:22
  15.6 0.8 collective-permute-done.3
  16.6 2.2 %collective-permute-done.2 = f32[2,6,2048]{2,0,1:T(2,128)S(1)} collective-permute-done((f32[2,6,2048]{2,0,1:T(2,128)S(1)}, f32[2,6,2048]{2,0,1:T(2,128)S(1)}, u32[]{:S(2)}, u32[]{:S(2)}) %collective-permute-start.2) | collective-permute-done | bytes 98336 | tf_op jit(solution)/shard_map/ppermute | solution.py:22
  19.2 0.2 fusion.70
  19.4 0.2 fusion.27
  20.0 0.2 fusion.50
  20.2 0.2 maximum_multiply_fusion
  20.5 0.2 fusion.74
  20.7 0.2 fusion.43
  20.9 0.2 slice_bitcast_fusion.4
  21.2 0.2 fusion.53
  21.4 0.2 maximum_multiply_fusion.1
  21.6 0.8 fusion.28
  22.5 0.2 fusion.72
  22.7 0.2 fusion.33
  23.5 2.0 %collective-permute-start.4 = (f32[3,32,2048]{2,1,0:T(8,128)S(1)}, f32[3,32,2048]{2,1,0:T(8,128)S(1)}, u32[]{:S(2)}, u32[]{:S(2)}) collective-permute-start(f32[3,32,2048]{2,1,0:T(8,128)S(1)} %maximum_multiply_fusion.2), channel_id=1, source_target_pairs={{0,8},{8,16},{16,24},{1,9},{9,17},{17,25},{2,10},{10,18},{18,26},{... | collective-permute-start | bytes 2359304 | tf_op jit(solution)/shard_map/ppermute | solution.py:31
  25.5 1.8 %collective-permute-done.4 = f32[3,32,2048]{2,1,0:T(8,128)S(1)} collective-permute-done((f32[3,32,2048]{2,1,0:T(8,128)S(1)}, f32[3,32,2048]{2,1,0:T(8,128)S(1)}, u32[]{:S(2)}, u32[]{:S(2)}) %collective-permute-start.4) | collective-permute-done | bytes 786464 | tf_op jit(solution)/shard_map/ppermute | solution.py:31
  27.3 1.0 subtract_bitcast_fusion
  28.3 6.9 %copy.110 = f32[1,3,32,2048]{2,0,1,3:T(1,128)S(1)} copy(f32[1,3,32,2048]{3,2,1,0:T(8,128)} %subtract_bitcast_fusion) | data formatting | bytes 1572864 | tf_op jit(solution)/shard_map/broadcast_in_dim | solution.py:109
  35.3 0.5 broadcast.212
  35.8 11.8 %reduce = f32[2048,3,32]{2,1,0:T(4,128)} reduce(f32[2048,3,1,32]{3,2,1,0:T(1,128)S(1)} %bitcast.127, f32[]{:T(128)} %broadcast.212), dimensions={2}, to_apply=%bitcast.125.reduce_sub_computation | reduce | bytes 1572868
  47.6 4.5 %reshape.290 = f32[4,1,49152]{2,1,0:T(1,128)S(1)} reshape(f32[2048,3,32]{2,1,0:T(4,128)} %reduce) | data formatting | bytes 1572864
  52.1 23.7 %all_to_all.33 = f32[4,1,49152]{2,1,0:T(1,128)S(1)} all-to-all(f32[4,1,49152]{2,1,0:T(1,128)S(1)} %reshape.290), channel_id=1, replica_groups=mesh['sub'=4,'tile'=8] {'sub'}, dimensions={0} | all-to-all | bytes 1572864 | tf_op jit(solution)/shard_map/all_to_all | solution.py:109
  75.8 3.8 %reduce.1 = f32[4,49152]{1,0:T(4,128)} reduce(f32[4,1,49152]{2,1,0:T(1,128)S(1)} %all_to_all.33, f32[]{:T(128)} %broadcast.212), dimensions={1}, to_apply=%all_to_all.24.reduce_sub_computation | reduce | bytes 1572868 | tf_op jit(solution)/shard_map/all_to_all | solution.py:109
  79.6 5.8 %reshape.291 = f32[2048,3,1,32]{3,2,1,0:T(1,128)S(1)} reshape(f32[4,49152]{1,0:T(4,128)} %reduce.1) | data formatting | bytes 1572864
  85.4 5.8 %copy.111 = f32[1,3,32,2048]{3,2,1,0:T(8,128)} copy(f32[1,3,32,2048]{2,0,1,3:T(1,128)S(1)} %bitcast.128) | data formatting | bytes 1572864 | tf_op jit(solution)/shard_map/all_to_all | solution.py:109
  91.2 1.7 %all_to_all.25 = f32[1,3,32,4,512]{4,3,2,1,0:T(4,128)S(1)} reshape(f32[1,3,32,2048]{3,2,1,0:T(8,128)} %copy.111) | data formatting | bytes 1572864 | tf_op jit(solution)/shard_map/all_to_all | solution.py:109
  92.9 1.5 %convolution_bitcast_fusion = f32[4,3,32,512]{3,0,2,1:T(4,128)S(1)} fusion(f32[1,3,32,4,512]{4,3,2,1,0:T(4,128)S(1)} %all_to_all.25, f32[4,4]{1,0:T(4,128)S(1)} %copy-done), kind=kOutput, calls=%fused_computation.3 | convolution fusion | flops 9437184 | bytes 1572928 | tf_op jit(solution)/shard_map/st,tfxy->sfxy/dot_general | solution.py:106
  94.4 0.3 copy.112
  94.6 14.0 %all_to_all.34 = f32[4,3,32,512]{3,2,1,0:T(8,128)S(1)} all-to-all(f32[4,3,32,512]{3,2,1,0:T(8,128)S(1)} %copy.112), channel_id=1, replica_groups=mesh['sub'=4,'tile'=8] {'sub'}, dimensions={0} | all-to-all | bytes 1572864 | tf_op jit(solution)/shard_map/all_to_all | solution.py:112
  108.7 0.5 copy.113
  109.2 0.5 squeeze.5
  109.8 4.4 %collective-permute-start.5 = (f32[3,3,2048]{2,1,0:T(4,128)S(1)}, f32[3,3,2048]{2,1,0:T(4,128)S(1)}, u32[]{:S(2)}, u32[]{:S(2)}) collective-permute-start(f32[3,3,2048]{2,1,0:T(4,128)S(1)} %get-tuple-element.24), channel_id=1, source_target_pairs={{0,1},{1,2},{2,3},{3,4},{4,5},{5,6},{6,7},{8,9},{9,10},{10,11},{11... | collective-permute-start | bytes 221192 | tf_op jit(solution)/shard_map/ppermute | solution.py:22
  114.1 1.5 %collective-permute-start.6 = (f32[3,3,2048]{2,1,0:T(4,128)S(1)}, f32[3,3,2048]{2,1,0:T(4,128)S(1)}, u32[]{:S(2)}, u32[]{:S(2)}) collective-permute-start(f32[3,3,2048]{2,1,0:T(4,128)S(1)} %get-tuple-element.25), channel_id=1, source_target_pairs={{1,0},{2,1},{3,2},{4,3},{5,4},{6,5},{7,6},{9,8},{10,9},{11,10},{12... | collective-permute-start | bytes 221192 | tf_op jit(solution)/shard_map/ppermute | solution.py:23
  115.7 1.0 slice_bitcast_fusion.1
  116.7 4.7 %collective-permute-done.6 = f32[3,3,2048]{2,1,0:T(4,128)S(1)} collective-permute-done((f32[3,3,2048]{2,1,0:T(4,128)S(1)}, f32[3,3,2048]{2,1,0:T(4,128)S(1)}, u32[]{:S(2)}, u32[]{:S(2)}) %collective-permute-start.6) | collective-permute-done | bytes 73760 | tf_op jit(solution)/shard_map/ppermute | solution.py:23
  121.6 0.4 fusion.66
  121.9 0.6 copy-done.3
  122.5 0.6 fusion.11
  123.2 0.4 fusion.64
  123.6 0.6 fusion.5
  124.3 0.3 fusion.62
  124.6 1.4 %fusion.20 = f32[1,3,32,2048]{3,2,1,0:T(8,128)} fusion(f32[3,34,2048]{2,1,0:T(8,128)S(1)} %fusion.5, f32[3,32,2047]{2,1,0:T(8,128)S(1)} %get-tuple-element.14, f32[3,32,1]{2,1,0:T(8,128)S(1)} %get-tuple-element.16, f32[3,32,1]{2,1,0:T(8,128)S(1)} %get-tuple-element.15, f32[3,32,2047]{2,1,0:T(8,128)S(1)} %get-tuple-element.13, ...), kind=kLoop, calls=%fused_computation.35 | loop fusion | flops 1966080 | bytes 4980864 | tf_op jit(solution)/shard_map/broadcast_in_dim | solution.py:120
  (42 shorter events, 2.5 us)
Async XLA Ops:
  0.0 92.9 %copy-start = (f32[4,4]{1,0:T(4,128)S(1)}, f32[4,4]{1,0:T(4,128)}, u32[]{:S(2)}) copy-start(f32[4,4]{1,0:T(4,128)} %param.9) | copy-start | bytes 196
  1.1 17.8 %copy-start.2 = (f32[1,3,32,2048]{3,2,1,0:T(8,128)S(1)}, f32[1,3,32,2048]{3,2,1,0:T(8,128)}, u32[]{:S(2)}) copy-start(f32[1,3,32,2048]{3,2,1,0:T(8,128)} %param.5) | copy-start | bytes 2359300
  1.1 17.8 %collective-permute-start = (f32[3,6,2048]{2,1,0:T(8,128)S(1)}, f32[3,6,2048]{2,1,0:T(8,128)S(1)}, u32[]{:S(2)}, u32[]{:S(2)}) collective-permute-start(f32[3,6,2048]{2,1,0:T(8,128)S(1)} %get-tuple-element.26), channel_id=1, source_target_pairs={{0,1},{1,2},{2,3},{3,4},{4,5},{5,6},{6,7},{8,9},{9,10},{10,11},{11... | collective-permute-start | bytes 442376 | tf_op jit(solution)/shard_map/ppermute | solution.py:22
  6.1 12.8 %collective-permute-start.1 = (f32[3,6,2048]{2,1,0:T(8,128)S(1)}, f32[3,6,2048]{2,1,0:T(8,128)S(1)}, u32[]{:S(2)}, u32[]{:S(2)}) collective-permute-start(f32[3,6,2048]{2,1,0:T(8,128)S(1)} %get-tuple-element.27), channel_id=1, source_target_pairs={{1,0},{2,1},{3,2},{4,3},{5,4},{6,5},{7,6},{9,8},{10,9},{11,10},{12... | collective-permute-start | bytes 442376 | tf_op jit(solution)/shard_map/ppermute | solution.py:23
  9.0 7.5 %collective-permute-start.3 = (f32[2,6,2048]{2,0,1:T(2,128)S(1)}, f32[2,6,2048]{2,0,1:T(2,128)S(1)}, u32[]{:S(2)}, u32[]{:S(2)}) collective-permute-start(f32[2,6,2048]{2,0,1:T(2,128)S(1)} %copy.116), channel_id=1, source_target_pairs={{1,0},{2,1},{3,2},{4,3},{5,4},{6,5},{7,6},{9,8},{10,9},{11,10},{12... | collective-permute-start | bytes 294920 | tf_op jit(solution)/shard_map/ppermute | solution.py:23
  10.4 8.3 %collective-permute-start.2 = (f32[2,6,2048]{2,0,1:T(2,128)S(1)}, f32[2,6,2048]{2,0,1:T(2,128)S(1)}, u32[]{:S(2)}, u32[]{:S(2)}) collective-permute-start(f32[2,6,2048]{2,0,1:T(2,128)S(1)} %copy.115), channel_id=1, source_target_pairs={{0,1},{1,2},{2,3},{3,4},{4,5},{5,6},{6,7},{8,9},{9,10},{10,11},{11... | collective-permute-start | bytes 294920 | tf_op jit(solution)/shard_map/ppermute | solution.py:22
  18.9 2.7 %copy-start.1 = (f32[2,44,2048]{2,1,0:T(8,128)}, f32[2,44,2048]{2,1,0:T(8,128)S(1)}, u32[]{:S(2)}) copy-start(f32[2,44,2048]{2,1,0:T(8,128)S(1)} %pad_maximum_fusion.6) | copy-start | bytes 2162692
  23.5 3.8 %collective-permute-start.4 = (f32[3,32,2048]{2,1,0:T(8,128)S(1)}, f32[3,32,2048]{2,1,0:T(8,128)S(1)}, u32[]{:S(2)}, u32[]{:S(2)}) collective-permute-start(f32[3,32,2048]{2,1,0:T(8,128)S(1)} %maximum_multiply_fusion.2), channel_id=1, source_target_pairs={{0,8},{8,16},{16,24},{1,9},{9,17},{17,25},{2,10},{10,18},{18,26},{... | collective-permute-start | bytes 2359304 | tf_op jit(solution)/shard_map/ppermute | solution.py:31
  109.8 6.9 %collective-permute-start.5 = (f32[3,3,2048]{2,1,0:T(4,128)S(1)}, f32[3,3,2048]{2,1,0:T(4,128)S(1)}, u32[]{:S(2)}, u32[]{:S(2)}) collective-permute-start(f32[3,3,2048]{2,1,0:T(4,128)S(1)} %get-tuple-element.24), channel_id=1, source_target_pairs={{0,1},{1,2},{2,3},{3,4},{4,5},{5,6},{6,7},{8,9},{9,10},{10,11},{11... | collective-permute-start | bytes 221192 | tf_op jit(solution)/shard_map/ppermute | solution.py:22
  114.1 7.3 %collective-permute-start.6 = (f32[3,3,2048]{2,1,0:T(4,128)S(1)}, f32[3,3,2048]{2,1,0:T(4,128)S(1)}, u32[]{:S(2)}, u32[]{:S(2)}) collective-permute-start(f32[3,3,2048]{2,1,0:T(4,128)S(1)} %get-tuple-element.25), channel_id=1, source_target_pairs={{1,0},{2,1},{3,2},{4,3},{5,4},{6,5},{7,6},{9,8},{10,9},{11,10},{12... | collective-permute-start | bytes 221192 | tf_op jit(solution)/shard_map/ppermute | solution.py:23
  121.6 1.0 copy-start.3
where the time goes:
time: 127 us; the launch traced here: 126 us
  blocking collectives  37.7 us (30%)
  local copies, waits for them, and re-layouts  32.1 us (25%)
  other arithmetic  23.9 us (19%)
  starting transfers between devices  20.7 us (16%)
  waiting for transfers between devices  9.57 us (8%)
  matrix products  1.45 us (1%)
    all_to_all x1, blocking collectives, local(): lax.all_to_all(jumps[None], 'sub', split_axis=3, concat_axis=0, tiled=True)  23.7 us
    ppermute x3, starting transfers between devices, with_halo(): before = lax.ppermute(last, axis, up)  14.6 us
    all_to_all x1, blocking collectives, local(): lax.all_to_all(mixed_parts, 'sub', split_axis=0, concat_axis=3, tiled=True)  14 us
    unnamed x1, other arithmetic  11.8 us
    unnamed x13, local copies, waits for them, and re-layouts  11.6 us
    all_to_all x2, local copies, waits for them, and re-layouts, local(): lax.all_to_all(jumps[None], 'sub', split_axis=3, concat_axis=0, tiled=True)  7.48 us
    broadcast_in_dim x1, local copies, waits for them, and re-layouts, local(): jumps[None]  6.94 us
    ppermute x3, waiting for transfers between devices, with_halo(): after = lax.ppermute(first, axis, down)  5.57 us
  transfers between devices with their start and end apart: 7, of which 4 were waited for; matrix products, arithmetic and copies ran while one was open for 2% of the time, Pallas kernels for 0%

commit v1 on v0

v1 whole, which is shorter than its diff:
```python
import functools

import jax
import jax.numpy as jnp
from jax import lax
from jax.experimental import pallas as pl
from jax.experimental.pallas import tpu as pltpu
from jax.sharding import PartitionSpec as P

FSTEPS = 3
DSTEPS = 3
time_step = 0.5
gravity = 1.0
coriolis = 0.3

PAD = 8
LANES = 128
FHALO = 2 * FSTEPS
CHUNK = 512


def kernel(
    subs, tiles, rows, cols, nclass,
    states, terrain, depth_tab, spread_tab, mixing, out,
    S, T, D, K, send_a, recv_a, send_b, recv_b, M,
    load_sem, halo_send, halo_recv, a_send, a_recv, b_send, b_recv, m_send, m_recv,
):
    pairs = subs // 2
    nch = cols // CHUNK
    me = lax.axis_index("sub")
    tile = lax.axis_index("tile")
    parity = lax.rem(me, 2)
    mate = me + 1 - 2 * parity
    pair = me // 2
    has_up = tile > 0
    has_down = tile < tiles - 1
    up, down = tile - 1, tile + 1

    loads = [
        pltpu.make_async_copy(states.at[0], S.at[:, pl.ds(PAD, rows), :], load_sem.at[0]),
        pltpu.make_async_copy(terrain, T.at[pl.ds(PAD, rows), :], load_sem.at[1]),
    ]
    for copy in loads:
        copy.start()

    barrier = pltpu.get_barrier_semaphore()
    pl.semaphore_signal(barrier, inc=1, device_id={"sub": mate})
    for k in range(1, pairs):
        pl.semaphore_signal(
            barrier, inc=1, device_id={"sub": lax.rem(pair + k, pairs) * 2 + parity}
        )

    @pl.when(has_up)
    def _():
        pl.semaphore_signal(barrier, inc=1, device_id={"tile": up})

    @pl.when(has_down)
    def _():
        pl.semaphore_signal(barrier, inc=1, device_id={"tile": down})

    pl.semaphore_wait(
        barrier, pairs + has_up.astype(jnp.int32) + has_down.astype(jnp.int32)
    )

    def halo_copy(source, target, index, where):
        return pltpu.make_async_remote_copy(
            src_ref=source, dst_ref=target, send_sem=halo_send.at[index],
            recv_sem=halo_recv.at[index], device_id={"tile": where},
            device_id_type=pl.DeviceIdType.MESH,
        )

    last, first = pl.ds(rows - FHALO, FHALO), pl.ds(0, FHALO)
    above, below = pl.ds(PAD - FHALO, FHALO), pl.ds(PAD + rows, FHALO)
    to_down = [
        halo_copy(terrain.at[last, :], T.at[above, :], 0, down),
        halo_copy(states.at[0, :, last, :], S.at[:, above, :], 1, down),
    ]
    to_up = [
        halo_copy(terrain.at[first, :], T.at[below, :], 2, up),
        halo_copy(states.at[0, :, first, :], S.at[:, below, :], 3, up),
    ]

    @pl.when(has_down)
    def _():
        for copy in to_down:
            copy.start()

    @pl.when(has_up)
    def _():
        for copy in to_up:
            copy.start()

    S[:, 0:PAD - FHALO, :] = jnp.zeros((3, PAD - FHALO, cols), jnp.float32)
    T[0:PAD - FHALO, :] = jnp.full((PAD - FHALO, cols), -1, jnp.int32)
    S[:, PAD + rows + FHALO:, :] = jnp.zeros((3, PAD - FHALO, cols), jnp.float32)
    T[PAD + rows + FHALO:, :] = jnp.full((PAD - FHALO, cols), -1, jnp.int32)
    M[:, 0:PAD - DSTEPS, :] = jnp.zeros((3, PAD - DSTEPS, cols), jnp.float32)
    M[:, PAD + rows + DSTEPS:, :] = jnp.zeros((3, PAD - DSTEPS, cols), jnp.float32)

    @pl.when(jnp.logical_not(has_up))
    def _():
        S[:, PAD - FHALO:PAD, :] = jnp.zeros((3, FHALO, cols), jnp.float32)
        T[PAD - FHALO:PAD, :] = jnp.full((FHALO, cols), -1, jnp.int32)
        M[:, PAD - DSTEPS:PAD, :] = jnp.zeros((3, DSTEPS, cols), jnp.float32)

    @pl.when(jnp.logical_not(has_down))
    def _():
        S[:, PAD + rows:PAD + rows + FHALO, :] = jnp.zeros((3, FHALO, cols), jnp.float32)
        T[PAD + rows:PAD + rows + FHALO, :] = jnp.full((FHALO, cols), -1, jnp.int32)
        M[:, PAD + rows:PAD + rows + DSTEPS, :] = jnp.zeros((3, DSTEPS, cols), jnp.float32)

    def lookup(start, count):
        for c in range(nch):
            span = pl.ds(c * CHUNK, CHUNK)
            kind = T[pl.ds(start, count), span]
            depth = jnp.zeros(kind.shape, jnp.float32)
            kappa = jnp.zeros(kind.shape, jnp.float32)
            for n in range(nclass):
                hit = kind == n
                depth = jnp.where(hit, depth_tab[n], depth)
                kappa = jnp.where(hit, spread_tab[n], kappa)
            D[pl.ds(start, count), span] = depth
            K[pl.ds(start, count), span] = kappa

    for copy in loads:
        copy.wait()
    lookup(PAD, rows)

    def wide(ref, lead, start, count, c):
        before = (c * CHUNK - LANES) % cols
        after = ((c + 1) * CHUNK) % cols
        return jnp.concatenate(
            [
                ref[lead + (pl.ds(start, count), pl.ds(before, LANES))],
                ref[lead + (pl.ds(start, count), pl.ds(c * CHUNK, CHUNK))],
                ref[lead + (pl.ds(start, count), pl.ds(after, LANES))],
            ],
            axis=-1,
        )

    def nxt(value, axis):
        return pltpu.roll(value, value.shape[axis] - 1, axis)

    def prv(value, axis):
        return pltpu.roll(value, 1, axis)

    def diff(value, axis):
        return nxt(value, axis) - prv(value, axis)

    def forward(start, count, c, masked):
        h, u, v = (wide(S, (f,), start, count, c) for f in range(3))
        d = wide(D, (), start, count, c)
        if masked:
            index = (
                tile * rows - PAD + start + lax.broadcasted_iota(jnp.int32, h.shape, 0)
            )
            inside = (index >= 0) & (index < tiles * rows)
        for _ in range(FSTEPS):
            new_h = h - (time_step * 0.5) * (diff(d * u, 0) + diff(d * v, 1))
            if masked:
                new_h = jnp.where(inside, new_h, 0.0)
            new_u = u - (time_step * gravity * 0.5) * diff(new_h, 0) + (time_step * coriolis) * v
            new_v = v - (time_step * gravity * 0.5) * diff(new_h, 1) - (time_step * coriolis) * u
            h, u, v = new_h, new_u, new_v
        return h, u, v

    later = jnp.minimum(me + 1, subs - 1)
    keep = jnp.where(me < subs - 1, 1.0, 0.0)

    def weights(s):
        return mixing[s, me], mixing[s, later] * keep

    dest_pair = [lax.rem(pair + k, pairs) for k in range(pairs)]
    w_mine = [weights(q * 2 + parity) for q in dest_pair]
    w_mate = [weights(q * 2 + 1 - parity) for q in dest_pair]

    edge = PAD
    inner = rows - 2 * edge
    blocks = {
        "inner": (edge, inner),
        "top": (0, edge),
        "bottom": (rows - edge, edge),
    }
    numbers = {"inner": 0, "top": 1, "bottom": 2}

    def a_copy(name, c, k):
        row, count = blocks[name]
        at = (k, slice(None), pl.ds(row, count), pl.ds(c * CHUNK, CHUNK))
        return pltpu.make_async_remote_copy(
            src_ref=send_a.at[at], dst_ref=recv_a.at[at],
            send_sem=a_send.at[k, numbers[name], c], recv_sem=a_recv.at[k, numbers[name], c],
            device_id={"sub": mate}, device_id_type=pl.DeviceIdType.MESH,
        )

    def b_copy(name, c, k):
        row, count = blocks[name]
        at = (k - 1, slice(None), pl.ds(row, count), pl.ds(c * CHUNK, CHUNK))
        return pltpu.make_async_remote_copy(
            src_ref=send_b.at[at], dst_ref=recv_b.at[at],
            send_sem=b_send.at[k - 1, numbers[name], c],
            recv_sem=b_recv.at[k - 1, numbers[name], c],
            device_id={"sub": dest_pair[k] * 2 + parity},
            device_id_type=pl.DeviceIdType.MESH,
        )

    def terms(name, c):
        row, count = blocks[name]
        if name == "inner":
            ends = forward(PAD, rows, c, False)
            skip = edge
        else:
            ends = forward(row, PAD + edge + PAD, c, True)
            skip = PAD
        span = pl.ds(c * CHUNK, CHUNK)
        order = list(range(1, pairs)) + [0]
        for k in order:
            for f in range(3):
                end = ends[f][skip:skip + count, LANES:LANES + CHUNK]
                start = S[f, pl.ds(PAD + row, count), span]
                a, b = w_mate[k]
                send_a[k, f, pl.ds(row, count), span] = a * start - b * end
                a, b = w_mine[k]
                mine = a * start - b * end
                if k == 0:
                    M[f, pl.ds(PAD + row, count), span] = mine
                else:
                    send_b[k - 1, f, pl.ds(row, count), span] = mine
            a_copy(name, c, k).start()

    def join(name, c):
        row, count = blocks[name]
        span = pl.ds(c * CHUNK, CHUNK)
        for k in list(range(1, pairs)) + [0]:
            a_copy(name, c, k).wait_recv()
            for f in range(3):
                got = recv_a[k, f, pl.ds(row, count), span]
                if k == 0:
                    at = (f, pl.ds(PAD + row, count), span)
                    M[at] = M[at] + got
                else:
                    at = (k - 1, f, pl.ds(row, count), span)
                    send_b[at] = send_b[at] + got
            if k > 0:
                b_copy(name, c, k).start()

    def finish(name, c):
        row, count = blocks[name]
        span = pl.ds(c * CHUNK, CHUNK)
        for k in range(1, pairs):
            b_copy(name, c, k).wait_recv()
        for f in range(3):
            at = (f, pl.ds(PAD + row, count), span)
            total = M[at]
            for k in range(1, pairs):
                total = total + recv_b[k - 1, f, pl.ds(row, count), span]
            M[at] = total

    def m_copy(way, c):
        span = pl.ds(c * CHUNK, CHUNK)
        if way == 0:
            source, target, where = pl.ds(PAD + rows - DSTEPS, DSTEPS), pl.ds(PAD - DSTEPS, DSTEPS), down
        else:
            source, target, where = pl.ds(PAD, DSTEPS), pl.ds(PAD + rows, DSTEPS), up
        return pltpu.make_async_remote_copy(
            src_ref=M.at[:, source, span], dst_ref=M.at[:, target, span],
            send_sem=m_send.at[way, c], recv_sem=m_recv.at[way, c],
            device_id={"tile": where}, device_id_type=pl.DeviceIdType.MESH,
        )

    def send_mixed(c):
        @pl.when(has_down)
        def _():
            m_copy(0, c).start()

        @pl.when(has_up)
        def _():
            m_copy(1, c).start()

    def take_mixed(c):
        @pl.when(has_up)
        def _():
            m_copy(0, c).wait_recv()

        @pl.when(has_down)
        def _():
            m_copy(1, c).wait_recv()

    def diffuse(c):
        total = rows + 2 * PAD
        kappa = wide(K, (), 0, total, c)
        for f in range(3):
            w = wide(M, (f,), 0, total, c)
            for _ in range(DSTEPS):
                near = nxt(w, 0) + prv(w, 0) + nxt(w, 1) + prv(w, 1)
                w = w + kappa * (near - 4.0 * w)
            out[0, f, :, pl.ds(c * CHUNK, CHUNK)] = w[PAD:PAD + rows, LANES:LANES + CHUNK]

    terms("inner", 0)
    for c in range(1, nch):
        terms("inner", c)
        join("inner", c - 1)
    join("inner", nch - 1)

    @pl.when(has_up)
    def _():
        for copy in to_down:
            copy.wait_recv()

    @pl.when(has_down)
    def _():
        for copy in to_up:
            copy.wait_recv()

    lookup(0, PAD)
    lookup(PAD + rows, PAD)

    def edge_terms(c):
        terms("top", c)
        terms("bottom", c)

    def edge_join(c):
        join("top", c)
        join("bottom", c)

    edge_terms(0)
    for c in range(1, nch):
        edge_terms(c)
        edge_join(c - 1)
    edge_join(nch - 1)
    for c in range(nch):
        finish("inner", c)
    done = []
    for c in range(nch):
        finish("top", c)
        finish("bottom", c)
        send_mixed(c)
        if c >= 2:
            if c == 2:
                take_mixed(0)
                take_mixed(1)
            take_mixed(c)
            if c < nch - 1 or nch == 3:
                diffuse(c - 1)
                done.append(c - 1)
    if nch <= 2:
        for c in range(nch):
            take_mixed(c)
    for c in range(nch):
        if c not in done:
            diffuse(c)

    for c in range(nch):
        for name in blocks:
            for k in range(pairs):
                a_copy(name, c, k).wait_send()
                if k > 0:
                    b_copy(name, c, k).wait_send()

    @pl.when(has_down)
    def _():
        for copy in to_down:
            copy.wait_send()
        for c in range(nch):
            m_copy(0, c).wait_send()

    @pl.when(has_up)
    def _():
        for copy in to_up:
            copy.wait_send()
        for c in range(nch):
            m_copy(1, c).wait_send()


def solution(mesh):
    subs, tiles = mesh.shape["sub"], mesh.shape["tile"]

    def local(states, terrain, depth_table, spread_table, mixing):
        _, fields, rows, cols = states.shape
        pairs = subs // 2
        nch = cols // CHUNK
        tall = rows + 2 * PAD
        dma = pltpu.SemaphoreType.DMA
        many = max(pairs - 1, 1)
        return pl.pallas_call(
            functools.partial(kernel, subs, tiles, rows, cols, depth_table.shape[0]),
            out_shape=jax.ShapeDtypeStruct(states.shape, jnp.float32),
            in_specs=[pl.BlockSpec(memory_space=pl.ANY)] * 2
            + [pl.BlockSpec(memory_space=pltpu.SMEM)] * 3,
            out_specs=pl.BlockSpec(memory_space=pltpu.VMEM),
            scratch_shapes=[
                pltpu.VMEM((fields, tall, cols), jnp.float32),
                pltpu.VMEM((tall, cols), jnp.int32),
                pltpu.VMEM((tall, cols), jnp.float32),
                pltpu.VMEM((tall, cols), jnp.float32),
                pltpu.VMEM((pairs, fields, rows, cols), jnp.float32),
                pltpu.VMEM((pairs, fields, rows, cols), jnp.float32),
                pltpu.VMEM((many, fields, rows, cols), jnp.float32),
                pltpu.VMEM((many, fields, rows, cols), jnp.float32),
                pltpu.VMEM((fields, tall, cols), jnp.float32),
                dma((2,)),
                dma((4,)),
                dma((4,)),
                dma((pairs, 3, nch)),
                dma((pairs, 3, nch)),
                dma((many, 3, nch)),
                dma((many, 3, nch)),
                dma((2, nch)),
                dma((2, nch)),
            ],
            compiler_params=pltpu.CompilerParams(
                collective_id=0, has_side_effects=True, vmem_limit_bytes=48 * 1024 * 1024
            ),
            name="gradient",
        )(states, terrain, depth_table, spread_table, mixing)

    in_specs = (P("sub", None, "tile", None), P("tile", None), P(), P(), P())
    out_specs = P("sub", None, "tile", None)
    return jax.shard_map(local, mesh=mesh, in_specs=in_specs, out_specs=out_specs, check_vma=False)
```

time: 127 us -> 42 us (0.33)
  blocking collectives: 37.7 us -> 0 us
  Pallas kernels: 0 us -> 36.8 us
  local copies, waits for them, and re-layouts: 32.1 us -> 4.95 us
  other arithmetic: 23.9 us -> 0 us
  starting transfers between devices: 20.7 us -> 0 us
  waiting for transfers between devices: 9.57 us -> 0 us
  matrix products: 1.45 us -> 0 us
    all_to_all x2 -> x0, blocking collectives: 37.7 us -> none  [the longest x1 23.7 us: local(): lax.all_to_all(jumps[None], 'sub', split_axis=3, concat_axis=0, tiled=True)]
    pallas_call x0 -> x1, Pallas kernels: none -> 36.8 us  [local(): pl.pallas_call(functools.partial(kernel, subs, tiles, rows, cols, depth_t...]
    ppermute x7 -> x0, starting transfers between devices: 20.7 us -> none  [the longest x3 14.6 us: with_halo(): before = lax.ppermute(last, axis, up)]
    unnamed x1 -> x0, other arithmetic: 11.8 us -> none
    ppermute x7 -> x0, waiting for transfers between devices: 9.57 us -> none  [the longest x3 5.57 us: with_halo(): after = lax.ppermute(first, axis, down)]
    all_to_all x3 -> x0, local copies, waits for them, and re-layouts: 7.99 us -> none  [the longest x2 7.48 us: local(): lax.all_to_all(jumps[None], 'sub', split_axis=3, concat_axis=0, tiled=True)]
    broadcast_in_dim x1 -> x0, local copies, waits for them, and re-layouts: 6.94 us -> none  [local(): jumps[None]]
    unnamed x13 -> x11, local copies, waits for them, and re-layouts: 11.6 us -> 4.95 us
  transfers between devices with their start and end apart: 7 -> 0, of which waited for: 4 -> 0; matrix products, arithmetic and copies ran while one was open for 2% -> 0% of each run, Pallas kernels for 0% -> 0%
where the time goes in v1:
time: 42 us; the launch traced here: 41.8 us
  Pallas kernels  36.8 us (88%)
  local copies, waits for them, and re-layouts  4.95 us (12%)
    pallas_call x1, Pallas kernels, local(): pl.pallas_call(functools.partial(kernel, subs, tiles, rows, cols, depth_t...  36.8 us
    unnamed x11, local copies, waits for them, and re-layouts  4.95 us

profile of v1, /device:TPU:0, one launch (start us, length us, event | category | flops | bytes accessed | tf_op | source)
XLA Modules:
  0.0 41.8 jit_solution(3586133827626523899)
XLA Ops:
  0.0 0.0 copy-start
  0.0 1.1 %copy-done = f32[1,3,32,2048]{3,2,1,0:T(8,128)S(1)} copy-done((f32[1,3,32,2048]{3,2,1,0:T(8,128)S(1)}, f32[1,3,32,2048]{3,2,1,0:T(8,128)}, u32[]{:S(2)}) %copy-start) | copy-done | bytes 786456
  1.1 0.0 copy-start.1
  1.1 0.9 %copy-done.1 = s32[32,2048]{1,0:T(8,128)S(1)} copy-done((s32[32,2048]{1,0:T(8,128)S(1)}, s32[32,2048]{1,0:T(8,128)}, u32[]{:S(2)}) %copy-start.1) | copy-done | bytes 262168
  2.1 0.0 copy-start.2
  2.1 0.7 %copy-done.2 = f32[4,4]{1,0:T(4,128)S(1)} copy-done((f32[4,4]{1,0:T(4,128)S(1)}, f32[4,4]{1,0:T(4,128)}, u32[]{:S(2)}) %copy-start.2) | copy-done | bytes 88
  2.8 0.0 copy-start.3
  2.8 0.7 %copy-done.3 = f32[8]{0:T(128)S(1)} copy-done((f32[8]{0:T(128)S(1)}, f32[8]{0:T(128)}, u32[]{:S(2)}) %copy-start.3) | copy-done | bytes 56
  3.4 0.0 copy-start.4
  3.4 0.7 %copy-done.4 = f32[8]{0:T(128)S(1)} copy-done((f32[8]{0:T(128)S(1)}, f32[8]{0:T(128)}, u32[]{:S(2)}) %copy-start.4) | copy-done | bytes 56
  4.1 36.8 %gradient.1 = f32[1,3,32,2048]{3,2,1,0:T(8,128)S(1)} custom-call(f32[1,3,32,2048]{3,2,1,0:T(8,128)S(1)} %copy-done, s32[32,2048]{1,0:T(8,128)S(1)} %copy-done.1, f32[8]{0:T(128)S(1)} %copy-done.3, f32[8]{0:T(128)S(1)} %copy-done.4, f32[4,4]{1,0:T(4,128)S(1)} %copy-done.2), custom_call_target="tpu_custom_call" | custom-call | tf_op jit(solution)/shard_map/gradient/pallas_call | solution.py:384
  40.9 0.9 %copy.7 = f32[1,3,32,2048]{3,2,1,0:T(8,128)} copy(f32[1,3,32,2048]{3,2,1,0:T(8,128)S(1)} %gradient.1) | data formatting | bytes 1572864
Async XLA Ops:
  0.0 1.1 %copy-start = (f32[1,3,32,2048]{3,2,1,0:T(8,128)S(1)}, f32[1,3,32,2048]{3,2,1,0:T(8,128)}, u32[]{:S(2)}) copy-start(f32[1,3,32,2048]{3,2,1,0:T(8,128)} %states.1) | copy-start | bytes 2359300
  1.1 0.9 %copy-start.1 = (s32[32,2048]{1,0:T(8,128)S(1)}, s32[32,2048]{1,0:T(8,128)}, u32[]{:S(2)}) copy-start(s32[32,2048]{1,0:T(8,128)} %terrain.1) | copy-start | bytes 786436
  2.1 0.7 %copy-start.2 = (f32[4,4]{1,0:T(4,128)S(1)}, f32[4,4]{1,0:T(4,128)}, u32[]{:S(2)}) copy-start(f32[4,4]{1,0:T(4,128)} %mixing.1) | copy-start | bytes 196
  2.8 0.7 %copy-start.3 = (f32[8]{0:T(128)S(1)}, f32[8]{0:T(128)}, u32[]{:S(2)}) copy-start(f32[8]{0:T(128)} %depth_tab.1) | copy-start | bytes 100
  3.4 0.7 %copy-start.4 = (f32[8]{0:T(128)S(1)}, f32[8]{0:T(128)}, u32[]{:S(2)}) copy-start(f32[8]{0:T(128)} %spread_tab.1) | copy-start | bytes 100

commit v2 on v1

--- a/solution.py
+++ b/solution.py
@@ -21,8 +21,8 @@
 
 def kernel(
     subs, tiles, rows, cols, nclass,
-    states, terrain, depth_tab, spread_tab, mixing, out,
-    S, T, D, K, send_a, recv_a, send_b, recv_b, M,
+    states, terrain, depth_in, spread_in, mixing_in, out,
+    depth_tab, spread_tab, mixing, S, T, D, K, send_a, recv_a, send_b, recv_b, M,
     load_sem, halo_send, halo_recv, a_send, a_recv, b_send, b_recv, m_send, m_recv,
 ):
     pairs = subs // 2
@@ -39,6 +39,9 @@
     loads = [
         pltpu.make_async_copy(states.at[0], S.at[:, pl.ds(PAD, rows), :], load_sem.at[0]),
         pltpu.make_async_copy(terrain, T.at[pl.ds(PAD, rows), :], load_sem.at[1]),
+        pltpu.make_async_copy(depth_in, depth_tab, load_sem.at[2]),
+        pltpu.make_async_copy(spread_in, spread_tab, load_sem.at[3]),
+        pltpu.make_async_copy(mixing_in, mixing, load_sem.at[4]),
     ]
     for copy in loads:
         copy.start()
@@ -64,31 +67,43 @@
 
     def halo_copy(source, target, index, where):
         return pltpu.make_async_remote_copy(
-            src_ref=source, dst_ref=target, send_sem=halo_send.at[index],
-            recv_sem=halo_recv.at[index], device_id={"tile": where},
+            src_ref=source, dst_ref=target, send_sem=halo_send.at[index[0], index[1]],
+            recv_sem=halo_recv.at[index[0], index[1]], device_id={"tile": where},
             device_id_type=pl.DeviceIdType.MESH,
         )
 
     last, first = pl.ds(rows - FHALO, FHALO), pl.ds(0, FHALO)
     above, below = pl.ds(PAD - FHALO, FHALO), pl.ds(PAD + rows, FHALO)
-    to_down = [
-        halo_copy(terrain.at[last, :], T.at[above, :], 0, down),
-        halo_copy(states.at[0, :, last, :], S.at[:, above, :], 1, down),
-    ]
-    to_up = [
-        halo_copy(terrain.at[first, :], T.at[below, :], 2, up),
-        halo_copy(states.at[0, :, first, :], S.at[:, below, :], 3, up),
-    ]
-
-    @pl.when(has_down)
-    def _():
-        for copy in to_down:
-            copy.start()
-
-    @pl.when(has_up)
-    def _():
-        for copy in to_up:
-            copy.start()
+    spans = [(cols - LANES, LANES)]
+    for c in range(nch):
+        begin = c * CHUNK + LANES if c > 0 else 0
+        spans.append((begin, min((c + 1) * CHUNK + LANES, cols - LANES) - begin))
+
+    def to_down(piece):
+        at = pl.ds(*spans[piece])
+        return [
+            halo_copy(terrain.at[last, at], T.at[above, at], (0, piece), down),
+            halo_copy(states.at[0, :, last, at], S.at[:, above, at], (1, piece), down),
+        ]
+
+    def to_up(piece):
+        at = pl.ds(*spans[piece])
+        return [
+            halo_copy(terrain.at[first, at], T.at[below, at], (2, piece), up),
+            halo_copy(states.at[0, :, first, at], S.at[:, below, at], (3, piece), up),
+        ]
+
+    for piece in range(nch + 1):
+
+        @pl.when(has_down)
+        def _():
+            for copy in to_down(piece):
+                copy.start()
+
+        @pl.when(has_up)
+        def _():
+            for copy in to_up(piece):
+                copy.start()
 
     S[:, 0:PAD - FHALO, :] = jnp.zeros((3, PAD - FHALO, cols), jnp.float32)
     T[0:PAD - FHALO, :] = jnp.full((PAD - FHALO, cols), -1, jnp.int32)
@@ -109,34 +124,45 @@
         T[PAD + rows:PAD + rows + FHALO, :] = jnp.full((FHALO, cols), -1, jnp.int32)
         M[:, PAD + rows:PAD + rows + DSTEPS, :] = jnp.zeros((3, DSTEPS, cols), jnp.float32)
 
-    def lookup(start, count):
-        for c in range(nch):
-            span = pl.ds(c * CHUNK, CHUNK)
-            kind = T[pl.ds(start, count), span]
-            depth = jnp.zeros(kind.shape, jnp.float32)
-            kappa = jnp.zeros(kind.shape, jnp.float32)
-            for n in range(nclass):
-                hit = kind == n
-                depth = jnp.where(hit, depth_tab[n], depth)
-                kappa = jnp.where(hit, spread_tab[n], kappa)
-            D[pl.ds(start, count), span] = depth
-            K[pl.ds(start, count), span] = kappa
+    def lookup(start, count, begin, width):
+        at = (pl.ds(start, count), pl.ds(begin, width))
+        kind = T[at]
+        depth = jnp.zeros(kind.shape, jnp.float32)
+        kappa = jnp.zeros(kind.shape, jnp.float32)
+        for n in range(nclass):
+            hit = kind == n
+            depth = jnp.where(hit, depth_tab[n], depth)
+            kappa = jnp.where(hit, spread_tab[n], kappa)
+        D[at] = depth
+        K[at] = kappa
+
+    def take_halo(piece):
+        @pl.when(has_up)
+        def _():
+            for copy in to_down(piece):
+                copy.wait_recv()
+
+        @pl.when(has_down)
+        def _():
+            for copy in to_up(piece):
+                copy.wait_recv()
+
+        lookup(0, PAD, *spans[piece])
+        lookup(PAD + rows, PAD, *spans[piece])
 
     for copy in loads:
         copy.wait()
-    lookup(PAD, rows)
-
-    def wide(ref, lead, start, count, c):
-        before = (c * CHUNK - LANES) % cols
-        after = ((c + 1) * CHUNK) % cols
-        return jnp.concatenate(
-            [
-                ref[lead + (pl.ds(start, count), pl.ds(before, LANES))],
-                ref[lead + (pl.ds(start, count), pl.ds(c * CHUNK, CHUNK))],
-                ref[lead + (pl.ds(start, count), pl.ds(after, LANES))],
-            ],
-            axis=-1,
-        )
+    for c in range(nch):
+        lookup(PAD, rows, c * CHUNK, CHUNK)
+
+    def wide(ref, lead, start, count, begin):
+        begin, width = (begin - LANES) % cols, CHUNK + 2 * LANES
+        parts = []
+        while width > 0:
+            size = min(width, cols - begin)
+            parts.append(ref[lead + (pl.ds(start, count), pl.ds(begin, size))])
+            begin, width = (begin + size) % cols, width - size
+        return parts[0] if len(parts) == 1 else jnp.concatenate(parts, axis=-1)
 
     def nxt(value, axis):
         return pltpu.roll(value, value.shape[axis] - 1, axis)
@@ -148,8 +174,8 @@
         return nxt(value, axis) - prv(value, axis)
 
     def forward(start, count, c, masked):
-        h, u, v = (wide(S, (f,), start, count, c) for f in range(3))
-        d = wide(D, (), start, count, c)
+        h, u, v = (wide(S, (f,), start, count, c * CHUNK) for f in range(3))
+        d = wide(D, (), start, count, c * CHUNK)
         if masked:
             index = (
                 tile * rows - PAD + start + lax.broadcasted_iota(jnp.int32, h.shape, 0)
@@ -286,68 +312,57 @@
             m_copy(1, c).wait_recv()
 
     def diffuse(c):
+        begin = c * CHUNK - LANES
         total = rows + 2 * PAD
-        kappa = wide(K, (), 0, total, c)
+        kappa = wide(K, (), 0, total, begin)
         for f in range(3):
-            w = wide(M, (f,), 0, total, c)
+            w = wide(M, (f,), 0, total, begin)
             for _ in range(DSTEPS):
                 near = nxt(w, 0) + prv(w, 0) + nxt(w, 1) + prv(w, 1)
                 w = w + kappa * (near - 4.0 * w)
-            out[0, f, :, pl.ds(c * CHUNK, CHUNK)] = w[PAD:PAD + rows, LANES:LANES + CHUNK]
+            w = w[PAD:PAD + rows, LANES:LANES + CHUNK]
+            if c > 0:
+                out[0, f, :, pl.ds(begin, CHUNK)] = w
+            else:
+                out[0, f, :, pl.ds(cols - LANES, LANES)] = w[:, :LANES]
+                out[0, f, :, pl.ds(0, CHUNK - LANES)] = w[:, LANES:]
+
+    def edge_terms(c):
+        take_halo(c + 1)
+        terms("top", c)
+        terms("bottom", c)
+
+    def edge_join(c):
+        join("top", c)
+        join("bottom", c)
 
     terms("inner", 0)
     for c in range(1, nch):
         terms("inner", c)
         join("inner", c - 1)
+    take_halo(0)
+    edge_terms(0)
     join("inner", nch - 1)
-
-    @pl.when(has_up)
-    def _():
-        for copy in to_down:
-            copy.wait_recv()
-
-    @pl.when(has_down)
-    def _():
-        for copy in to_up:
-            copy.wait_recv()
-
-    lookup(0, PAD)
-    lookup(PAD + rows, PAD)
-
-    def edge_terms(c):
-        terms("top", c)
-        terms("bottom", c)
-
-    def edge_join(c):
-        join("top", c)
-        join("bottom", c)
-
-    edge_terms(0)
     for c in range(1, nch):
         edge_terms(c)
         edge_join(c - 1)
     edge_join(nch - 1)
     for c in range(nch):
         finish("inner", c)
-    done = []
     for c in range(nch):
         finish("top", c)
         finish("bottom", c)
         send_mixed(c)
         if c >= 2:
+            take_mixed(c - 1)
             if c == 2:
                 take_mixed(0)
-                take_mixed(1)
-            take_mixed(c)
-            if c < nch - 1 or nch == 3:
-                diffuse(c - 1)
-                done.append(c - 1)
-    if nch <= 2:
-        for c in range(nch):
-            take_mixed(c)
-    for c in range(nch):
-        if c not in done:
-            diffuse(c)
+            diffuse(c - 1)
+    take_mixed(nch - 1)
+    if nch == 2:
+        take_mixed(0)
+    diffuse(nch - 1)
+    diffuse(0)
 
     for c in range(nch):
         for name in blocks:
@@ -358,15 +373,17 @@
 
     @pl.when(has_down)
     def _():
-        for copy in to_down:
-            copy.wait_send()
+        for piece in range(nch + 1):
+            for copy in to_down(piece):
+                copy.wait_send()
         for c in range(nch):
             m_copy(0, c).wait_send()
 
     @pl.when(has_up)
     def _():
-        for copy in to_up:
-            copy.wait_send()
+        for piece in range(nch + 1):
+            for copy in to_up(piece):
+                copy.wait_send()
         for c in range(nch):
             m_copy(1, c).wait_send()
 
@@ -384,10 +401,12 @@
         return pl.pallas_call(
             functools.partial(kernel, subs, tiles, rows, cols, depth_table.shape[0]),
             out_shape=jax.ShapeDtypeStruct(states.shape, jnp.float32),
-            in_specs=[pl.BlockSpec(memory_space=pl.ANY)] * 2
-            + [pl.BlockSpec(memory_space=pltpu.SMEM)] * 3,
+            in_specs=[pl.BlockSpec(memory_space=pltpu.HBM)] * 5,
             out_specs=pl.BlockSpec(memory_space=pltpu.VMEM),
             scratch_shapes=[
+                pltpu.SMEM(depth_table.shape, jnp.float32),
+                pltpu.SMEM(spread_table.shape, jnp.float32),
+                pltpu.SMEM(mixing.shape, jnp.float32),
                 pltpu.VMEM((fields, tall, cols), jnp.float32),
                 pltpu.VMEM((tall, cols), jnp.int32),
                 pltpu.VMEM((tall, cols), jnp.float32),
@@ -397,9 +416,9 @@
                 pltpu.VMEM((many, fields, rows, cols), jnp.float32),
                 pltpu.VMEM((many, fields, rows, cols), jnp.float32),
                 pltpu.VMEM((fields, tall, cols), jnp.float32),
-                dma((2,)),
-                dma((4,)),
-                dma((4,)),
+                dma((5,)),
+                dma((4, nch + 1)),
+                dma((4, nch + 1)),
                 dma((pairs, 3, nch)),
                 dma((pairs, 3, nch)),
                 dma((many, 3, nch)),
@@ -408,7 +427,7 @@
                 dma((2, nch)),
             ],
             compiler_params=pltpu.CompilerParams(
-                collective_id=0, has_side_effects=True, vmem_limit_bytes=48 * 1024 * 1024
+                collective_id=0, has_side_effects=True, vmem_limit_bytes=67043328
             ),
             name="gradient",
         )(states, terrain, depth_table, spread_table, mixing)

time: 42 us -> 35.4 us (0.84)
  Pallas kernels: 36.8 us -> 33.2 us
  local copies, waits for them, and re-layouts: 4.95 us -> 2.06 us
    pallas_call x1, Pallas kernels: 36.8 us -> 33.2 us  [local(): pl.pallas_call(functools.partial(kernel, subs, tiles, rows, cols, depth_t...]
    unnamed x11 -> x1, local copies, waits for them, and re-layouts: 4.95 us -> 2.06 us
where the time goes in v2:
time: 35.4 us; the launch traced here: 35.3 us
  Pallas kernels  33.2 us (94%)
  local copies, waits for them, and re-layouts  2.06 us (6%)
    pallas_call x1, Pallas kernels, local(): pl.pallas_call(functools.partial(kernel, subs, tiles, rows, cols, depth_t...  33.2 us
    unnamed x1, local copies, waits for them, and re-layouts  2.06 us

profile of v2, /device:TPU:0, one launch (start us, length us, event | category | flops | bytes accessed | tf_op | source)
XLA Modules:
  0.0 35.3 jit_solution(3836850370870879108)
XLA Ops:
  0.0 33.2 %gradient.1 = f32[1,3,32,2048]{3,2,1,0:T(8,128)} custom-call(f32[1,3,32,2048]{3,2,1,0:T(8,128)} %states.1, s32[32,2048]{1,0:T(8,128)} %terrain.1, f32[8]{0:T(128)} %depth_in.1, f32[8]{0:T(128)} %spread_in.1, f32[4,4]{1,0:T(4,128)} %mixing_in.1), custom_call_target="tpu_custom_call" | custom-call | tf_op jit(solution)/shard_map/gradient/pallas_call | solution.py:401
  33.2 2.1 %copy.7 = f32[1,3,32,2048]{3,2,1,0:T(8,128)} copy(f32[1,3,32,2048]{3,2,1,0:T(8,128)} %gradient.1) | data formatting | bytes 1572864

commit v3 on v2

--- a/solution.py
+++ b/solution.py
@@ -427,10 +427,10 @@
                 dma((2, nch)),
             ],
             compiler_params=pltpu.CompilerParams(
-                collective_id=0, has_side_effects=True, vmem_limit_bytes=67043328
+                collective_id=0, has_side_effects=True, vmem_limit_bytes=48 * 1024 * 1024
             ),
             name="gradient",
-        )(states, terrain, depth_table, spread_table, mixing)
+        )(*(pltpu.with_memory_space_constraint(value, pltpu.HBM) for value in (states, terrain, depth_table, spread_table, mixing)))
 
     in_specs = (P("sub", None, "tile", None), P("tile", None), P(), P(), P())
     out_specs = P("sub", None, "tile", None)

time: 35.4 us -> 33.3 us (0.941)
  local copies, waits for them, and re-layouts: 2.06 us -> 0.88 us
  Pallas kernels: 33.2 us -> 32.3 us
    unnamed x1, local copies, waits for them, and re-layouts: 2.06 us -> 0.88 us
    pallas_call x1, Pallas kernels: 33.2 us -> 32.3 us  [local(): pl.pallas_call(functools.partial(kernel, subs, tiles, rows, cols, depth_t...]
where the time goes in v3:
time: 33.3 us; the launch traced here: 33.2 us
  Pallas kernels  32.3 us (97%)
  local copies, waits for them, and re-layouts  0.88 us (3%)
    pallas_call x1, Pallas kernels, local(): pl.pallas_call(functools.partial(kernel, subs, tiles, rows, cols, depth_t...  32.3 us
    unnamed x1, local copies, waits for them, and re-layouts  0.88 us

profile of v3, /device:TPU:0, one launch (start us, length us, event | category | flops | bytes accessed | tf_op | source)
XLA Modules:
  0.0 33.2 jit_solution(17456152128867360306)
XLA Ops:
  0.0 32.3 %gradient.1 = f32[1,3,32,2048]{3,2,1,0:T(8,128)S(1)} custom-call(f32[1,3,32,2048]{3,2,1,0:T(8,128)} %states.1, s32[32,2048]{1,0:T(8,128)} %terrain.1, f32[8]{0:T(128)} %depth_in.1, f32[8]{0:T(128)} %spread_in.1, f32[4,4]{1,0:T(4,128)} %mixing_in.1), custom_call_target="tpu_custom_call" | custom-call | tf_op jit(solution)/shard_map/gradient/pallas_call | solution.py:401
  32.3 0.9 %copy.7 = f32[1,3,32,2048]{3,2,1,0:T(8,128)} copy(f32[1,3,32,2048]{3,2,1,0:T(8,128)S(1)} %gradient.1) | data formatting | bytes 1572864

commit v4 on v3

--- a/solution.py
+++ b/solution.py
@@ -346,9 +346,9 @@
     for c in range(1, nch):
         edge_terms(c)
         edge_join(c - 1)
+        finish("inner", c - 1)
     edge_join(nch - 1)
-    for c in range(nch):
-        finish("inner", c)
+    finish("inner", nch - 1)
     for c in range(nch):
         finish("top", c)
         finish("bottom", c)

time: 33.3 us -> 33.3 us (level)
  no operation moved by 1% of the time
where the time goes in v4:
time: 33.3 us; the launch traced here: 33.2 us
  Pallas kernels  32.3 us (97%)
  local copies, waits for them, and re-layouts  0.88 us (3%)
    pallas_call x1, Pallas kernels, local(): pl.pallas_call(functools.partial(kernel, subs, tiles, rows, cols, depth_t...  32.3 us
    unnamed x1, local copies, waits for them, and re-layouts  0.88 us

profile of v4, /device:TPU:0, one launch (start us, length us, event | category | flops | bytes accessed | tf_op | source)
XLA Modules:
  0.0 33.2 jit_solution(5113450882468759086)
XLA Ops:
  0.0 32.3 %gradient.1 = f32[1,3,32,2048]{3,2,1,0:T(8,128)S(1)} custom-call(f32[1,3,32,2048]{3,2,1,0:T(8,128)} %states.1, s32[32,2048]{1,0:T(8,128)} %terrain.1, f32[8]{0:T(128)} %depth_in.1, f32[8]{0:T(128)} %spread_in.1, f32[4,4]{1,0:T(4,128)} %mixing_in.1), custom_call_target="tpu_custom_call" | custom-call | tf_op jit(solution)/shard_map/gradient/pallas_call | solution.py:401
  32.3 0.9 %copy.7 = f32[1,3,32,2048]{3,2,1,0:T(8,128)} copy(f32[1,3,32,2048]{3,2,1,0:T(8,128)S(1)} %gradient.1) | data formatting | bytes 1572864
